TPU v7x, 32 devices: a whole 2x2x4 slice. The times are simulated.
32 devices in a mesh: dp: 8 (over z, x), sp: 4 (over y, core).
Axes of the slice: x: 2, y: 2, z: 4, core: 2. Of those that a mesh axis runs over, the one named last changes fastest.
Arguments:
- hidden_in: bfloat16 [8, 1024, 512], P('dp', 'sp'), may hold values from -6 to 6
- cotangent: float32 [8, 1024, 512], P('dp', 'sp'), may hold values from -6 to 6
- lengths: int32 [8], P('dp'), may hold values from 256 to 1024, as said below
- master: float32 [6301696], P(('dp', 'sp'))
- moment_one: float32 [6301696], P(('dp', 'sp'))
- moment_two: float32 [6301696], P(('dp', 'sp'))
Outputs:
- output: float32 [8, 1024, 512], P('dp', 'sp')
- input_grad: float32 [8, 1024, 512], P('dp', 'sp')
- new_master: float32 [6301696], P(('dp', 'sp'))
- new_moment_one: float32 [6301696], P(('dp', 'sp'))
- new_moment_two: float32 [6301696], P(('dp', 'sp'))
- new_weights: bfloat16 [6301696], P(('dp', 'sp'))
- grad_norm: float32 [], replicated
- gains_grad: float32 [2, 2, 512], replicated
Inputs may be any that keep to these rules, and one draw needn't show every extreme that they name: `lengths`: in every draw one sequence has all 1024 tokens real and another only 256.
All inputs are finite; a program needn't handle non-finite values.
Results may differ from a plain program's by a relative error of at most 0.017.
Values may be sent and summed in bfloat16 or wider, within the bound.
A program may use at most 192 MiB of HBM per device.

v0:
```python
import jax
import jax.numpy as jnp
from jax import lax
from jax.sharding import PartitionSpec as P

D = 512
HEADS = 8
HEAD_DIM = 64
FF = 1368
SEQ = 1024
BLOCK = 512
STEP = 5
NORM_EPS = 1e-06
ADAM_EPS = 1e-08
LEARN_RATE = 0.02
DECAY_RATE = 0.01


def shortened(array):

    def short(part):
        return part.astype(jnp.bfloat16) if part.dtype == jnp.float32 else part

    return jax.tree.map(short, array)


def layer_pieces(flat_weights, layer_index):
    shapes = [(D, 3 * D), (D, D), (D, 2 * FF), (FF, D), (2, D)]
    offset = layer_index * (4 * D * D + 3 * D * FF + 2 * D)
    pieces = []
    for dims_pair in shapes:
        length_now = dims_pair[0] * dims_pair[1]
        pieces.append(flat_weights[offset : offset + length_now].reshape(dims_pair))
        offset = offset + length_now
    return pieces


def rope_tables(positions):
    half_dim = HEAD_DIM // 2
    frequency = jnp.exp(
        -jnp.log(10000.0) * jnp.arange(half_dim).astype(jnp.float32) * 2.0 / HEAD_DIM
    )
    angles = positions.astype(jnp.float32)[:, None] * frequency[None, :]
    return (jnp.cos(angles), jnp.sin(angles))


def rotate(values, cosine_table, sine_table):
    half_dim = values.shape[-1] // 2
    first_half = values[..., :half_dim]
    second_half = values[..., half_dim:]
    cos_rows = cosine_table[:, None, :]
    sin_rows = sine_table[:, None, :]
    return jnp.concatenate(
        [
            first_half * cos_rows - second_half * sin_rows,
            second_half * cos_rows + first_half * sin_rows,
        ],
        axis=-1,
    )


def unrotate(values, cosine_table, sine_table):
    half_dim = values.shape[-1] // 2
    first_half = values[..., :half_dim]
    second_half = values[..., half_dim:]
    cos_rows = cosine_table[:, None, :]
    sin_rows = sine_table[:, None, :]
    return jnp.concatenate(
        [
            first_half * cos_rows + second_half * sin_rows,
            second_half * cos_rows - first_half * sin_rows,
        ],
        axis=-1,
    )


def norm_forward(stream, gain):
    factor = lax.rsqrt(jnp.mean(stream * stream, axis=-1, keepdims=True) + NORM_EPS)
    return (stream * factor * gain, factor)


def norm_backward(upstream, stream, factor, gain):
    scaled = upstream * gain
    gain_grad = jnp.sum(upstream * stream * factor, axis=(0, 1))
    stream_grad = factor * scaled - stream * factor**3 * jnp.mean(
        scaled * stream, axis=-1, keepdims=True
    )
    return (stream_grad, gain_grad)


def block_logits(query_block, key_rows, offset, length_now):
    raw_scores = jnp.einsum(
        "qhd,khd->hqk", query_block, key_rows, preferred_element_type=jnp.float32
    )
    row_place = offset + jnp.arange(query_block.shape[0])[:, None]
    col_place = jnp.arange(key_rows.shape[0])[None, :]
    allowed = (col_place <= row_place) & (col_place < length_now)
    return jnp.where(allowed[None], raw_scores * HEAD_DIM ** (-0.5), -1000000000.0)


def attend_forward(packed_in):
    sequence, length_now = packed_in
    query_rows = sequence[:, 0]
    key_rows = sequence[:, 1]
    value_rows = sequence[:, 2]
    context_parts = []
    logsum_parts = []
    for offset in range(0, SEQ, BLOCK):
        logits = block_logits(query_rows[offset : offset + BLOCK], key_rows, offset, length_now)
        logsum = jax.nn.logsumexp(logits, axis=-1)
        weights_soft = jnp.exp(logits - logsum[..., None]).astype(jnp.bfloat16)
        context_parts.append(
            jnp.einsum("hqk,khd->qhd", weights_soft, value_rows, preferred_element_type=jnp.float32)
        )
        logsum_parts.append(logsum)
    return (jnp.concatenate(context_parts, 0), jnp.concatenate(logsum_parts, 1))


def attend_backward(packed_in):
    sequence, grad_context, logsum, length_now = packed_in
    query_rows = sequence[:, 0]
    key_rows = sequence[:, 1]
    value_rows = sequence[:, 2]
    grad_rows = grad_context.reshape(query_rows.shape)
    key_grad = jnp.zeros(key_rows.shape, jnp.float32)
    value_grad = jnp.zeros(value_rows.shape, jnp.float32)
    query_parts = []
    for offset in range(0, SEQ, BLOCK):
        query_block = query_rows[offset : offset + BLOCK]
        grad_block = grad_rows[offset : offset + BLOCK]
        logits = block_logits(query_block, key_rows, offset, length_now)
        weights_soft = jnp.exp(logits - logsum[:, offset : offset + BLOCK, None])
        value_grad = value_grad + jnp.einsum(
            "hqk,qhd->khd",
            weights_soft.astype(jnp.bfloat16),
            grad_block,
            preferred_element_type=jnp.float32,
        )
        weight_grad = jnp.einsum(
            "qhd,khd->hqk", grad_block, value_rows, preferred_element_type=jnp.float32
        )
        centered = weight_grad - jnp.sum(weights_soft * weight_grad, axis=-1, keepdims=True)
        score_grad = (weights_soft * centered * HEAD_DIM ** (-0.5)).astype(jnp.bfloat16)
        query_parts.append(
            jnp.einsum("hqk,khd->qhd", score_grad, key_rows, preferred_element_type=jnp.float32)
        )
        key_grad = key_grad + jnp.einsum(
            "hqk,qhd->khd", score_grad, query_block, preferred_element_type=jnp.float32
        )
    query_grad = jnp.concatenate(query_parts, 0)
    return jnp.stack([query_grad, key_grad, value_grad], axis=1).astype(jnp.bfloat16)


def attention_forward(stream, weight_qkv, weight_out, cosine_table, sine_table, lengths):
    seq_count, row_count, feature_count = stream.shape
    groups = lax.axis_size("sp")
    head_local = HEADS // groups
    inputs_low = stream.astype(jnp.bfloat16).reshape(-1, feature_count)
    projected = jnp.dot(inputs_low, weight_qkv, preferred_element_type=jnp.float32).reshape(
        seq_count, row_count, 3, HEADS, HEAD_DIM
    )
    rotated = jnp.stack(
        [
            rotate(projected[:, :, 0], cosine_table, sine_table),
            rotate(projected[:, :, 1], cosine_table, sine_table),
            projected[:, :, 2],
        ],
        axis=2,
    )
    outgoing = rotated.astype(jnp.bfloat16).reshape(
        seq_count, row_count, 3, groups, head_local * HEAD_DIM
    )
    by_heads = lax.all_to_all(outgoing, "sp", split_axis=3, concat_axis=1, tiled=True)
    by_heads = by_heads.reshape(seq_count, row_count * groups, 3, head_local, HEAD_DIM)
    context, logsum = lax.map(attend_forward, (by_heads, lengths))
    context_low = context.astype(jnp.bfloat16).reshape(
        seq_count, row_count * groups, 1, head_local * HEAD_DIM
    )
    by_tokens = lax.all_to_all(context_low, "sp", split_axis=1, concat_axis=2, tiled=True)
    context_rows = by_tokens.reshape(-1, feature_count)
    branch = jnp.dot(context_rows, weight_out, preferred_element_type=jnp.float32).reshape(
        seq_count, row_count, feature_count
    )
    return (branch, (inputs_low, context_rows, by_heads, logsum))


def attention_backward(upstream, saved, weight_qkv, weight_out, cosine_table, sine_table, lengths):
    inputs_low, context_rows, by_heads, logsum = saved
    seq_count, row_count, feature_count = upstream.shape
    groups = lax.axis_size("sp")
    head_local = HEADS // groups
    upstream_low = upstream.astype(jnp.bfloat16).reshape(-1, feature_count)
    out_grad = jnp.einsum(
        "nd,ne->de", context_rows, upstream_low, preferred_element_type=jnp.float32
    )
    context_grad = jnp.dot(upstream_low, weight_out.T, preferred_element_type=jnp.float32).astype(
        jnp.bfloat16
    )
    context_grad = context_grad.reshape(seq_count, row_count, groups, head_local * HEAD_DIM)
    grad_heads = lax.all_to_all(context_grad, "sp", split_axis=2, concat_axis=1, tiled=True)
    head_grads = lax.map(attend_backward, (by_heads, grad_heads, logsum, lengths))
    outgoing = head_grads.reshape(seq_count, row_count * groups, 3, 1, head_local * HEAD_DIM)
    token_grads = lax.all_to_all(
        shortened(outgoing), "sp", split_axis=1, concat_axis=3, tiled=True
    ).astype(outgoing.dtype)
    token_grads = token_grads.reshape(seq_count, row_count, 3, HEADS, HEAD_DIM).astype(jnp.float32)
    lin_grad = jnp.stack(
        [
            unrotate(token_grads[:, :, 0], cosine_table, sine_table),
            unrotate(token_grads[:, :, 1], cosine_table, sine_table),
            token_grads[:, :, 2],
        ],
        axis=2,
    )
    lin_grad = lin_grad.astype(jnp.bfloat16).reshape(-1, 3 * feature_count)
    qkv_grad = jnp.einsum("nd,ne->de", inputs_low, lin_grad, preferred_element_type=jnp.float32)
    input_grad = jnp.dot(lin_grad, weight_qkv.T, preferred_element_type=jnp.float32).reshape(
        seq_count, row_count, feature_count
    )
    return (input_grad, qkv_grad, out_grad)


def ffn_forward(stream, weight_gu, weight_down):
    seq_count, row_count, feature_count = stream.shape
    inputs_low = stream.astype(jnp.bfloat16).reshape(-1, feature_count)
    both_parts = jnp.dot(inputs_low, weight_gu, preferred_element_type=jnp.float32)
    units = (jax.nn.silu(both_parts[:, :FF]) * both_parts[:, FF:]).astype(jnp.bfloat16)
    branch = jnp.dot(units, weight_down, preferred_element_type=jnp.float32).reshape(
        seq_count, row_count, feature_count
    )
    return (branch, (inputs_low, both_parts, units))


def ffn_backward(upstream, saved, weight_gu, weight_down):
    inputs_low, both_parts, units = saved
    seq_count, row_count, feature_count = upstream.shape
    upstream_low = upstream.astype(jnp.bfloat16).reshape(-1, feature_count)
    down_grad = jnp.einsum("nf,nd->fd", units, upstream_low, preferred_element_type=jnp.float32)
    units_grad = jnp.dot(upstream_low, weight_down.T, preferred_element_type=jnp.float32)
    gate_part = both_parts[:, :FF]
    up_part = both_parts[:, FF:]
    sigmoid_part = jax.nn.sigmoid(gate_part)
    gate_grad = units_grad * up_part * sigmoid_part * (1.0 + gate_part * (1.0 - sigmoid_part))
    up_grad = units_grad * gate_part * sigmoid_part
    both_grad = jnp.concatenate([gate_grad, up_grad], axis=1).astype(jnp.bfloat16)
    gu_grad = jnp.einsum("nd,nf->df", inputs_low, both_grad, preferred_element_type=jnp.float32)
    input_grad = jnp.dot(both_grad, weight_gu.T, preferred_element_type=jnp.float32).reshape(
        seq_count, row_count, feature_count
    )
    return (input_grad, gu_grad, down_grad)


def shards(hidden_in, cotangent, lengths, master, moment_one, moment_two):
    shard_low = master.astype(jnp.bfloat16)
    flat_weights = lax.all_gather(shard_low, ("dp", "sp"), axis=0, tiled=True)
    seq_count, row_count, feature_count = hidden_in.shape
    positions = lax.axis_index("sp") * row_count + jnp.arange(row_count)
    cosine_table, sine_table = rope_tables(positions)
    first_weights = layer_pieces(flat_weights, 0)
    second_weights = layer_pieces(flat_weights, 1)
    gains_first = first_weights[4].astype(jnp.float32)
    gains_second = second_weights[4].astype(jnp.float32)
    stream_zero = hidden_in.astype(jnp.float32)
    attn_zero, attn_zero_saved = attention_forward(
        stream_zero, first_weights[0], first_weights[1], cosine_table, sine_table, lengths
    )
    resid_one = stream_zero + attn_zero
    stream_one, factor_one = norm_forward(resid_one, gains_first[0])
    ffn_zero, ffn_zero_saved = ffn_forward(stream_one, first_weights[2], first_weights[3])
    resid_two = stream_one + ffn_zero
    stream_two, factor_two = norm_forward(resid_two, gains_first[1])
    normed_three, factor_three = norm_forward(stream_two, gains_second[0])
    attn_one, attn_one_saved = attention_forward(
        normed_three, second_weights[0], second_weights[1], cosine_table, sine_table, lengths
    )
    stream_three = stream_two + attn_one
    normed_four, factor_four = norm_forward(stream_three, gains_second[1])
    ffn_one, ffn_one_saved = ffn_forward(normed_four, second_weights[2], second_weights[3])
    output = stream_three + ffn_one
    keep = (positions[None, :] < lengths[:, None]).astype(jnp.float32)
    upstream = cotangent * keep[:, :, None]
    ffn_in_grad, gu_grad_one, down_grad_one = ffn_backward(
        upstream, ffn_one_saved, second_weights[2], second_weights[3]
    )
    norm_part, gain_grad_four = norm_backward(
        ffn_in_grad, stream_three, factor_four, gains_second[1]
    )
    three_grad = upstream + norm_part
    attn_in_grad, qkv_grad_one, out_grad_one = attention_backward(
        three_grad,
        attn_one_saved,
        second_weights[0],
        second_weights[1],
        cosine_table,
        sine_table,
        lengths,
    )
    norm_part, gain_grad_three = norm_backward(
        attn_in_grad, stream_two, factor_three, gains_second[0]
    )
    two_grad = three_grad + norm_part
    resid_two_grad, gain_grad_two = norm_backward(two_grad, resid_two, factor_two, gains_first[1])
    ffn_in_grad, gu_grad_zero, down_grad_zero = ffn_backward(
        resid_two_grad, ffn_zero_saved, first_weights[2], first_weights[3]
    )
    one_grad = resid_two_grad + ffn_in_grad
    resid_one_grad, gain_grad_one = norm_backward(one_grad, resid_one, factor_one, gains_first[0])
    attn_in_grad, qkv_grad_zero, out_grad_zero = attention_backward(
        resid_one_grad,
        attn_zero_saved,
        first_weights[0],
        first_weights[1],
        cosine_table,
        sine_table,
        lengths,
    )
    input_grad = resid_one_grad + attn_in_grad
    gains_first_grad = jnp.stack([gain_grad_one, gain_grad_two])
    gains_second_grad = jnp.stack([gain_grad_three, gain_grad_four])
    grad_flat = jnp.concatenate(
        [
            qkv_grad_zero.reshape(-1),
            out_grad_zero.reshape(-1),
            gu_grad_zero.reshape(-1),
            down_grad_zero.reshape(-1),
            gains_first_grad.reshape(-1),
            qkv_grad_one.reshape(-1),
            out_grad_one.reshape(-1),
            gu_grad_one.reshape(-1),
            down_grad_one.reshape(-1),
            gains_second_grad.reshape(-1),
        ]
    )
    grad_grid = grad_flat.reshape(lax.axis_size("dp"), lax.axis_size("sp"), -1)
    partial_sum = lax.psum_scatter(
        grad_grid.astype(jnp.bfloat16), "sp", scatter_dimension=1, tiled=True
    ).astype(jnp.float32)
    grad_shard = lax.psum_scatter(partial_sum, "dp", scatter_dimension=0, tiled=True).reshape(-1)
    gains_local = jnp.stack([gains_first_grad, gains_second_grad])
    squares, gains_grad = lax.psum((jnp.sum(grad_shard * grad_shard), gains_local), ("dp", "sp"))
    grad_norm = jnp.sqrt(squares)
    clipped = grad_shard * jnp.minimum(1.0, 1.0 / grad_norm)
    new_one = 0.5 * moment_one + 0.5 * clipped
    new_two = 0.5 * moment_two + 0.5 * clipped * clipped
    correction = 1.0 - 0.5**STEP
    new_master = master * (1.0 - LEARN_RATE * DECAY_RATE) - LEARN_RATE * (new_one / correction) / (
        jnp.sqrt(new_two / correction) + ADAM_EPS
    )
    return (
        output,
        input_grad,
        new_master,
        new_one,
        new_two,
        new_master.astype(jnp.bfloat16),
        grad_norm,
        gains_grad,
    )


def solution(mesh):
    in_specs = (
        P("dp", "sp", None),
        P("dp", "sp", None),
        P("dp"),
        P(("dp", "sp")),
        P(("dp", "sp")),
        P(("dp", "sp")),
    )
    out_specs = (
        P("dp", "sp", None),
        P("dp", "sp", None),
        P(("dp", "sp")),
        P(("dp", "sp")),
        P(("dp", "sp")),
        P(("dp", "sp")),
        P(),
        P(),
    )
    return jax.shard_map(shards, mesh=mesh, in_specs=in_specs, out_specs=out_specs, check_vma=False)
```

profile of v0, /device:TPU:12, one launch (start us, length us, event | category | flops | bytes accessed | tf_op | source)
XLA Modules:
  0.0 1094.7 jit_solution(13723838610632103288)
XLA Ops:
  8.4 4.7 broadcast.325
  13.1 7.3 dynamic-update-slice
  22.6 230.5 %all-reduce.7.cloned.1.call-done = bf16[6301696]{0:T(1024)(128)(2,1)} async-done(((bf16[6301696]{0:T(1024)(128)(2,1)}), bf16[6301696]{0:T(1024)(128)(2,1)}) %all-reduce.7.cloned.1.call-update) | async-done | bytes 12603408
  253.1 3.8 fusion.190
  265.3 4.7 all-to-all-start
  270.0 3.9 fusion.188
  279.6 4.2 reshape.1051
  286.4 5.8 reshape.1048
  293.6 13.9 %slice.340 = bf16[1368,512]{1,0:T(8,128)(2,1)} reshape(bf16[700416]{0:T(1024)(128)(2,1)} %get-tuple-element.90) | data formatting | bytes 2801664 | tf_op jit(solution)/shard_map/slice | solution.py:33
  325.7 4.4 all-to-all-done.1
  337.8 14.3 %all_to_all.108 = bf16[1,256,3,4,128]{1,4,2,0,3:T(8,128)(2,1)S(1)} all-to-all(bf16[1,256,3,4,128]{1,4,2,0,3:T(8,128)(2,1)S(1)} %pad_maximum_fusion.9), channel_id=1, replica_groups=mesh['dp'=8,'sp'=4] {'sp'}, dimensions={3} | all-to-all | bytes 1572864 | tf_op jit(solution)/shard_map/all_to_all | solution.py:173
  373.9 6.1 all-to-all-start.3
  381.3 7.2 reshape.1055
  407.6 7.6 all_to_all.109
  419.3 4.4 fusion.105
  423.7 3.8 fusion.143
  427.5 12.8 %fusion.22 = f32[2,64,1024]{2,1,0:T(8,128)} fusion(f32[2,512,1024]{2,1,0:T(8,128)} %fusion.143, bf16[1024,3,2,64]{0,3,2,1:T(8,128)(2,1)} %squeeze.98, f32[2,512,1024]{2,1,0:T(8,128)} %get-tuple-element.167, f32[2,512]{1,0:T(2,128)S(1)} %log_add_fusion.1, pred[512,1024]{1,0:T(8,128)(4,1)S(1)} %copy-done.23), kind=kOutput, calls=%fused_computation.39 | convolution fusion | flops 145754112 | bytes 18489344 | tf_op jit(solution)/shard_map/while/body/eval_jaxpr/hqk,qhd->khd/dot_general | solution.py:147
  440.3 12.5 %fusion.91 = bf16[512,2,64]{0,2,1:T(8,128)(2,1)} fusion(f32[2,512,1024]{2,1,0:T(8,128)} %fusion.143, bf16[1024,3,2,64]{0,3,2,1:T(8,128)(2,1)} %squeeze.98, f32[2,512,1024]{2,1,0:T(8,128)} %get-tuple-element.167, f32[2,512]{1,0:T(2,128)S(1)} %log_add_fusion.1, pred[512,1024]{1,0:T(8,128)(4,1)S(1)} %copy-done.23), kind=kOutput, calls=%fused_computation.109 | convolution fusion | flops 145819648 | bytes 18227200 | tf_op jit(solution)/shard_map/while/body/eval_jaxpr/hqk,khd->qhd/dot_general | solution.py:145
  456.1 3.8 fusion.142
  465.3 12.2 %fusion.94 = bf16[512,2,64]{0,2,1:T(8,128)(2,1)} fusion(f32[2,512,1024]{2,1,0:T(8,128)} %fusion.142, bf16[1024,3,2,64]{0,3,2,1:T(8,128)(2,1)} %squeeze.98, f32[2,512,1024]{2,1,0:T(8,128)} %copy-done.31, f32[2,512]{1,0:T(2,128)S(1)} %log_add_fusion, pred[512,1024]{1,0:T(8,128)(4,1)S(1)} %copy-done.22), kind=kOutput, calls=%fused_computation.110 | convolution fusion | flops 145819648 | bytes 18227200 | tf_op jit(solution)/shard_map/while/body/eval_jaxpr/hqk,khd->qhd/dot_general | solution.py:145
  477.5 12.6 %fusion.73 = bf16[2,64,1024]{2,1,0:T(8,128)(2,1)} fusion(f32[2,64,1024]{2,1,0:T(8,128)} %fusion.22, f32[2,512,1024]{2,1,0:T(8,128)} %fusion.142, bf16[1024,3,2,64]{0,3,2,1:T(8,128)(2,1)} %squeeze.98, f32[2,512,1024]{2,1,0:T(8,128)} %copy-done.31, f32[2,512]{1,0:T(2,128)S(1)} %log_add_fusion, pred[512,1024]{1,0:T(8,128)(4,1)S(1)} %copy-done.22), kind=kOutput, calls=%fused_computation.95 | convolution fusion | flops 146016256 | bytes 18751488 | tf_op jit(solution)/shard_map/while/body/eval_jaxpr/hqk,qhd->khd/dot_general | solution.py:147
  495.7 4.1 pad_maximum_fusion.2
  499.8 6.3 all-to-all-start.5
  508.4 3.8 convolution_convert_fusion
  512.2 4.5 copy.134
  516.7 6.4 reshape.1072
  544.7 4.2 all-to-all-start.6
  548.9 3.9 convolution_convert_fusion.1
  555.7 3.6 fusion.110
  559.3 3.7 fusion.139
  563.0 13.1 %fusion.34 = f32[2,64,1024]{2,1,0:T(8,128)} fusion(f32[2,512,1024]{2,1,0:T(8,128)} %fusion.139, bf16[1024,3,2,64]{0,3,2,1:T(8,128)(2,1)} %copy-done.41, f32[2,512,1024]{2,1,0:T(8,128)} %copy-done.30, f32[2,512]{1,0:T(2,128)S(1)} %log_add_fusion.3, pred[512,1024]{1,0:T(8,128)(4,1)} %get-tuple-element.154), kind=kOutput, calls=%fused_computation.43 | convolution fusion | flops 145754112 | bytes 18489344 | tf_op jit(solution)/shard_map/while/body/eval_jaxpr/hqk,qhd->khd/dot_general | solution.py:147
  576.1 12.8 %fusion.97 = bf16[512,2,64]{0,2,1:T(8,128)(2,1)} fusion(f32[2,512,1024]{2,1,0:T(8,128)} %fusion.139, bf16[1024,3,2,64]{0,3,2,1:T(8,128)(2,1)} %copy-done.41, f32[2,512,1024]{2,1,0:T(8,128)} %copy-done.30, f32[2,512]{1,0:T(2,128)S(1)} %log_add_fusion.3, pred[512,1024]{1,0:T(8,128)(4,1)} %get-tuple-element.154), kind=kOutput, calls=%fused_computation.111 | convolution fusion | flops 145819648 | bytes 18227200 | tf_op jit(solution)/shard_map/while/body/eval_jaxpr/hqk,khd->qhd/dot_general | solution.py:145
  589.2 3.8 fusion.138
  595.0 12.3 %fusion.100 = bf16[512,2,64]{0,2,1:T(8,128)(2,1)} fusion(f32[2,512,1024]{2,1,0:T(8,128)} %fusion.138, bf16[1024,3,2,64]{0,3,2,1:T(8,128)(2,1)} %copy-done.41, f32[2,512,1024]{2,1,0:T(8,128)} %copy-done.28, f32[2,512]{1,0:T(2,128)S(1)} %log_add_fusion.2, pred[512,1024]{1,0:T(8,128)(4,1)S(1)} %copy-done.22), kind=kOutput, calls=%fused_computation.112 | convolution fusion | flops 145819648 | bytes 18227200 | tf_op jit(solution)/shard_map/while/body/eval_jaxpr/hqk,khd->qhd/dot_general | solution.py:145
  607.3 12.0 %fusion.76 = bf16[2,64,1024]{2,1,0:T(8,128)(2,1)S(1)} fusion(f32[2,64,1024]{2,1,0:T(8,128)} %fusion.34, f32[2,512,1024]{2,1,0:T(8,128)} %fusion.138, bf16[1024,3,2,64]{0,3,2,1:T(8,128)(2,1)} %copy-done.41, f32[2,512,1024]{2,1,0:T(8,128)} %copy-done.28, f32[2,512]{1,0:T(2,128)S(1)} %log_add_fusion.2, pred[512,1024]{1,0:T(8,128)(4,1)S(1)} %copy-done.22), kind=kOutput, calls=%fused_computation.96 | convolution fusion | flops 146016256 | bytes 18751488 | tf_op jit(solution)/shard_map/while/body/eval_jaxpr/hqk,qhd->khd/dot_general | solution.py:147
  621.7 3.8 pad_maximum_fusion.3
  625.6 4.6 all-to-all-start.7
  631.5 5.0 copy.133
  636.5 6.5 reshape.1067
  653.9 4.4 reshape.1065
  672.0 23.6 %convert_element_type.303 = bf16[8,4,196928]{2,1,0:T(4,128)(2,1)} reshape(bf16[6301696]{0:T(1024)(128)(2,1)} %constant_dynamic-update-slice_fusion) | data formatting | bytes 25206784 | tf_op jit(solution)/shard_map/convert_element_type | solution.py:336
  695.6 11.5 %copy.135 = bf16[8,4,196928]{2,0,1:T(8,128)(2,1)} copy(bf16[8,4,196928]{2,1,0:T(4,128)(2,1)} %convert_element_type.303) | data formatting | bytes 25206784 | tf_op jit(solution)/shard_map/convert_element_type | solution.py:336
  707.2 98.9 %reduce-scatter.4.cloned.1.call-done = bf16[8,1,196928]{2,0,1:T(8,128)(2,1)} async-done(((bf16[8,4,196928]{2,0,1:T(8,128)(2,1)}), bf16[8,1,196928]{2,0,1:T(8,128)(2,1)}) %reduce-scatter.4.cloned.1.call-update) | async-done | bytes 3150864
  806.1 6.9 copy.136
  817.3 208.4 %all-reduce.9.cloned.1.call-done = f32[8,1,196928]{2,1,0:T(1,128)} async-done(((f32[8,1,196928]{2,1,0:T(1,128)}), f32[8,1,196928]{2,1,0:T(1,128)}) %all-reduce.9.cloned.1.call-update) | async-done | bytes 6301712
  1025.7 3.9 multiply_reduce_fusion.5
  1031.0 42.5 %all-reduce.3 = (f32[]{:T(128)}, f32[2,2,512]{2,1,0:T(2,128)}) all-reduce(f32[]{:T(128)} %multiply_reduce_fusion.5, f32[2,2,512]{2,1,0:T(2,128)S(1)} %pad_maximum_fusion.20), channel_id=1, replica_groups=mesh['dp'=8,'sp'=4] {'dp','sp'}, use_global_device_ids=true, to_apply=%region_27.28 | all-reduce | flops 2049 | bytes 16392 | tf_op jit(solution)/shard_map/psum | solution.py:340
  1074.3 9.0 multiply_reduce_fusion.4
  (293 shorter events, 172.9 us)
Async XLA Ops:
  7.2 245.9 %all-reduce.7.cloned.1.call-start = ((), (), s32[]{:S(2)}) async-start(), calls=%async_computation.9 | async-start | bytes 25206784
  22.6 340.1 %copy-start.21 = (pred[512,1024]{1,0:T(8,128)(4,1)}, pred[512,1024]{1,0:T(8,128)(4,1)S(1)}, u32[]{:S(2)}) copy-start(pred[512,1024]{1,0:T(8,128)(4,1)S(1)} %get-tuple-element.155) | copy-start | bytes 1572868
  256.9 5.1 copy-start.38
  260.2 3.9 copy-start
  265.3 42.9 %all-to-all-start = ((bf16[1,256,3,4,128]{1,4,2,0,3:T(8,128)(2,1)}), bf16[1,256,3,4,128]{1,4,2,0,3:T(8,128)(2,1)}, u32[]{:S(2)}, u32[]{:S(2)}) async-start(bf16[1,256,3,4,128]{1,4,2,0,3:T(8,128)(2,1)} %pad_maximum_fusion.8), calls=%async_computation | async-start | bytes 1572864 | tf_op jit(solution)/shard_map/all_to_all | solution.py:173
  293.6 37.0 %copy-start.26 = (bf16[512,512]{1,0:T(8,128)(2,1)}, bf16[512,512]{1,0:T(8,128)(2,1)S(1)}, u32[]{:S(2)}) copy-start(bf16[512,512]{1,0:T(8,128)(2,1)S(1)} %slice.333) | copy-start | bytes 1572868
  310.5 6.1 copy-start.41
  311.6 2.5 copy-start.28
  315.4 2.5 copy-start.30
  317.9 12.7 %copy-start.39 = (bf16[1,256,512]{2,1,0:T(8,128)(2,1)S(1)}, bf16[1,256,512]{2,1,0:T(8,128)(2,1)}, u32[]{:S(2)}) copy-start(bf16[1,256,512]{2,1,0:T(8,128)(2,1)} %param.6) | copy-start | bytes 786436
  322.3 7.8 all-to-all-start.1
  330.6 4.2 copy-start.36
  331.0 3.8 copy-start.17
  334.3 3.1 copy-start.4
  334.3 2.4 copy-start.14
  358.3 4.5 copy-start.31
  364.2 3.6 copy-start.33
  373.9 18.2 %all-to-all-start.3 = ((bf16[4,2,16384]{2,1,0:T(2,128)(2,1)}), bf16[4,2,16384]{2,1,0:T(2,128)(2,1)}, u32[]{:S(2)}, u32[]{:S(2)}) async-start(bf16[4,2,16384]{2,1,0:T(2,128)(2,1)} %reshape.1086), calls=%async_computation.3 | async-start | bytes 524288 | tf_op jit(solution)/shard_map/all_to_all | solution.py:179
  381.3 14.5 %copy-start.24 = (bf16[512,512]{1,0:T(8,128)(2,1)}, bf16[512,512]{1,0:T(8,128)(2,1)S(1)}, u32[]{:S(2)}) copy-start(bf16[512,512]{1,0:T(8,128)(2,1)S(1)} %slice.359) | copy-start | bytes 1572868
  395.8 4.7 copy-start.15
  395.8 4.7 copy-start.43
  419.3 4.4 copy-start.52
  452.7 7.2 copy-start.22
  456.1 3.8 copy-start.32
  456.1 3.9 copy-start.51
  499.8 27.0 %all-to-all-start.5 = ((bf16[1,1024,3,1,128]{4,2,3,0,1:T(4,128)(2,1)}), bf16[1,1024,3,1,128]{4,2,3,0,1:T(4,128)(2,1)}, u32[]{:S(2)}, u32[]{:S(2)}) async-start(bf16[1,1024,3,1,128]{4,2,3,0,1:T(4,128)(2,1)} %pad_maximum_fusion.2), calls=%async_computation.5 | async-start | bytes 2097152 | tf_op jit(solution)/shard_map/all_to_all | solution.py:203
  534.1 2.5 copy-start.18
  537.5 2.7 copy-start.49
  537.5 2.7 copy-start.50
  540.2 90.0 %copy-start.8 = (f32[1,256,512]{2,1,0:T(8,128)}, f32[1,256,512]{2,1,0:T(8,128)S(1)}, u32[]{:S(2)}) copy-start(f32[1,256,512]{2,1,0:T(8,128)S(1)} %multiply_subtract_fusion) | copy-start | bytes 1572868
  544.7 9.8 all-to-all-start.6
  548.9 3.9 copy-start.46
  589.2 3.8 copy-start.29
  619.2 10.9 copy-start.37
  625.6 23.0 %all-to-all-start.7 = ((bf16[1,1024,3,1,128]{4,2,3,0,1:T(4,128)(2,1)}), bf16[1,1024,3,1,128]{4,2,3,0,1:T(4,128)(2,1)}, u32[]{:S(2)}, u32[]{:S(2)}) async-start(bf16[1,1024,3,1,128]{4,2,3,0,1:T(4,128)(2,1)} %pad_maximum_fusion.3), calls=%async_computation.7 | async-start | bytes 2097152 | tf_op jit(solution)/shard_map/all_to_all | solution.py:203
  630.2 175.9 %reduce-scatter.4.cloned.1.call-start = ((), (), s32[]{:S(2)}) async-start(), calls=%async_computation.11 | async-start | bytes 15759360
  636.4 6.5 copy-start.16
  636.4 8.4 copy-start.35
  653.9 9.1 copy-start.7
  658.4 6.4 copy-start.20
  663.1 3.4 copy-start.13
  664.8 3.0 copy-start.44
  664.8 3.9 copy-start.6
  666.5 3.8 copy-start.19
  707.2 318.5 %all-reduce.9.cloned.1.call-start = ((), (), s32[]{:S(2)}) async-start(), calls=%async_computation.10 | async-start | bytes 12607488
  813.0 216.5 %copy-start.1 = (bf16[512,1536]{1,0:T(8,128)(2,1)S(1)}, bf16[512,1536]{1,0:T(8,128)(2,1)}, u32[]{:S(2)}) copy-start(bf16[512,1536]{1,0:T(8,128)(2,1)} %copy-done) | copy-start | bytes 4718596
  813.0 216.5 %copy-start.9 = (f32[1,256,512]{2,1,0:T(8,128)S(1)}, f32[1,256,512]{2,1,0:T(8,128)}, u32[]{:S(2)}) copy-start(f32[1,256,512]{2,1,0:T(8,128)} %copy-done.8) | copy-start | bytes 1572868
  813.0 216.5 %copy-start.11 = (bf16[1,256,3,8,64]{1,4,3,2,0:T(8,128)(2,1)S(1)}, bf16[1,256,3,8,64]{1,4,3,2,0:T(8,128)(2,1)}, u32[]{:S(2)}) copy-start(bf16[1,256,3,8,64]{1,4,3,2,0:T(8,128)(2,1)} %copy-done.10) | copy-start | bytes 2359300
  (15 other events, 22.5 us)
Sparse Core Ops, SparseCore 0:
  20.5 232.5 all-reduce.6
  707.3 98.7 reduce-scatter.3
  813.2 212.4 all-reduce.8
where the time goes:
time: 1100 us; the launch traced here: 1090 us
  waiting for transfers between devices  542 us (49%)
  local copies, waits for them, and re-layouts  213 us (19%)
  matrix products  180 us (16%)
  blocking collectives  64.4 us (6%)
  other arithmetic  48.7 us (4%)
  starting transfers between devices  29.4 us (3%)
  between operations  17.7 us (2%)
    unnamed x6, waiting for transfers between devices  538 us
    dot_general x4, matrix products, attend_backward(): jnp.einsum('hqk,qhd->khd', score_grad, query_block, preferred_element_typ...  50.6 us
    dot_general x4, matrix products, attend_backward(): jnp.einsum('hqk,khd->qhd', score_grad, key_rows, preferred_element_type=j...  49.8 us
    psum x1, blocking collectives, shards(): lax.psum((jnp.sum(grad_shard * grad_shard), gains_local), ('dp', 'sp'))  42.5 us
    unnamed x133, local copies, waits for them, and re-layouts  40.7 us
    convert_element_type x2, local copies, waits for them, and re-layouts, shards(): grad_grid.astype(jnp.bfloat16)  35.1 us
    slice x8, local copies, waits for them, and re-layouts, layer_pieces(): pieces.append(flat_weights[offset:offset + length_now].reshape(dims_pair))  33.5 us
  transfers between devices with their start and end apart: 9, of which 4 were waited for; matrix products, arithmetic and copies ran while one was open for 9% of the time, Pallas kernels for 0%

commit v1 on v0

--- a/solution.py
+++ b/solution.py
@@ -251,6 +251,11 @@
 
 
 def shards(hidden_in, cotangent, lengths, master, moment_one, moment_two):
+
+    def list_grid_in(vec):
+        x_new = lax.psum(vec, axis_name="sp")
+        return lax.psum(x_new, axis_name="dp")
+
     shard_low = master.astype(jnp.bfloat16)
     flat_weights = lax.all_gather(shard_low, ("dp", "sp"), axis=0, tiled=True)
     seq_count, row_count, feature_count = hidden_in.shape
@@ -337,7 +342,7 @@
     ).astype(jnp.float32)
     grad_shard = lax.psum_scatter(partial_sum, "dp", scatter_dimension=0, tiled=True).reshape(-1)
     gains_local = jnp.stack([gains_first_grad, gains_second_grad])
-    squares, gains_grad = lax.psum((jnp.sum(grad_shard * grad_shard), gains_local), ("dp", "sp"))
+    squares, gains_grad = list_grid_in((jnp.sum(grad_shard * grad_shard), gains_local))
     grad_norm = jnp.sqrt(squares)
     clipped = grad_shard * jnp.minimum(1.0, 1.0 / grad_norm)
     new_one = 0.5 * moment_one + 0.5 * clipped

time: 1100 us -> 1090 us (level)
  blocking collectives: 64.4 us -> 48.1 us
    psum x1 -> x2, blocking collectives: 42.5 us -> 26.2 us  [the longest x1 19.4 us: list_grid_in(): return lax.psum(x_new, axis_name='dp')]
    unnamed x133 -> x131, local copies, waits for them, and re-layouts: 40.7 us -> 40.7 us
where the time goes in v1:
time: 1090 us; the launch traced here: 1080 us
  waiting for transfers between devices  542 us (50%)
  local copies, waits for them, and re-layouts  210 us (19%)
  matrix products  180 us (17%)
  other arithmetic  48.8 us (4%)
  blocking collectives  48.1 us (4%)
  starting transfers between devices  29.4 us (3%)
  between operations  17.7 us (2%)
    unnamed x6, waiting for transfers between devices  538 us
    dot_general x4, matrix products, attend_backward(): jnp.einsum('hqk,qhd->khd', score_grad, query_block, preferred_element_typ...  50.9 us
    dot_general x4, matrix products, attend_backward(): jnp.einsum('hqk,khd->qhd', score_grad, key_rows, preferred_element_type=j...  50.1 us
    unnamed x131, local copies, waits for them, and re-layouts  40.7 us
    convert_element_type x2, local copies, waits for them, and re-layouts, shards(): grad_grid.astype(jnp.bfloat16)  35.1 us
    slice x8, local copies, waits for them, and re-layouts, layer_pieces(): pieces.append(flat_weights[offset:offset + length_now].reshape(dims_pair))  33.1 us
  transfers between devices with their start and end apart: 9, of which 4 were waited for; matrix products, arithmetic and copies ran while one was open for 9% of the time, Pallas kernels for 0%

profile of v1, /device:TPU:12, one launch (start us, length us, event | category | flops | bytes accessed | tf_op | source)
XLA Modules:
  0.0 1076.2 jit_solution(3178908968413588736)
XLA Ops:
  8.4 4.7 broadcast.325
  13.1 7.3 dynamic-update-slice
  22.8 230.3 %all-reduce.8.cloned.1.call-done = bf16[6301696]{0:T(1024)(128)(2,1)} async-done(((bf16[6301696]{0:T(1024)(128)(2,1)}), bf16[6301696]{0:T(1024)(128)(2,1)}) %all-reduce.8.cloned.1.call-update) | async-done | bytes 12603408
  260.8 4.7 all-to-all-start
  265.4 3.9 fusion.188
  275.1 4.3 reshape.1051
  281.9 5.8 reshape.1048
  289.2 13.9 %slice.340 = bf16[1368,512]{1,0:T(8,128)(2,1)} reshape(bf16[700416]{0:T(1024)(128)(2,1)} %get-tuple-element.92) | data formatting | bytes 2801664 | tf_op jit(solution)/shard_map/slice | solution.py:33
  321.3 4.4 all-to-all-done.1
  333.4 14.3 %all_to_all.108 = bf16[1,256,3,4,128]{1,4,2,0,3:T(8,128)(2,1)S(1)} all-to-all(bf16[1,256,3,4,128]{1,4,2,0,3:T(8,128)(2,1)S(1)} %pad_maximum_fusion.9), channel_id=1, replica_groups=mesh['dp'=8,'sp'=4] {'sp'}, dimensions={3} | all-to-all | bytes 1572864 | tf_op jit(solution)/shard_map/all_to_all | solution.py:173
  371.0 6.1 all-to-all-start.3
  378.5 7.2 reshape.1055
  404.8 7.6 all_to_all.109
  416.4 4.4 fusion.105
  420.9 3.8 fusion.143
  424.6 13.2 %fusion.22 = f32[2,64,1024]{2,1,0:T(8,128)} fusion(f32[2,512,1024]{2,1,0:T(8,128)} %fusion.143, bf16[1024,3,2,64]{0,3,2,1:T(8,128)(2,1)} %squeeze.98, f32[2,512,1024]{2,1,0:T(8,128)} %get-tuple-element.169, f32[2,512]{1,0:T(2,128)S(1)} %log_add_fusion.1, pred[512,1024]{1,0:T(8,128)(4,1)} %get-tuple-element.156), kind=kOutput, calls=%fused_computation.39 | convolution fusion | flops 145754112 | bytes 18489344 | tf_op jit(solution)/shard_map/while/body/eval_jaxpr/hqk,qhd->khd/dot_general | solution.py:147
  437.9 12.8 %fusion.91 = bf16[512,2,64]{0,2,1:T(8,128)(2,1)} fusion(f32[2,512,1024]{2,1,0:T(8,128)} %fusion.143, bf16[1024,3,2,64]{0,3,2,1:T(8,128)(2,1)} %squeeze.98, f32[2,512,1024]{2,1,0:T(8,128)} %get-tuple-element.169, f32[2,512]{1,0:T(2,128)S(1)} %log_add_fusion.1, pred[512,1024]{1,0:T(8,128)(4,1)} %get-tuple-element.156), kind=kOutput, calls=%fused_computation.109 | convolution fusion | flops 145819648 | bytes 18227200 | tf_op jit(solution)/shard_map/while/body/eval_jaxpr/hqk,khd->qhd/dot_general | solution.py:145
  454.0 3.9 fusion.142
  463.1 12.2 %fusion.94 = bf16[512,2,64]{0,2,1:T(8,128)(2,1)} fusion(f32[2,512,1024]{2,1,0:T(8,128)} %fusion.142, bf16[1024,3,2,64]{0,3,2,1:T(8,128)(2,1)} %squeeze.98, f32[2,512,1024]{2,1,0:T(8,128)} %copy-done.30, f32[2,512]{1,0:T(2,128)S(1)} %log_add_fusion, pred[512,1024]{1,0:T(8,128)(4,1)S(1)} %copy-done.21), kind=kOutput, calls=%fused_computation.110 | convolution fusion | flops 145819648 | bytes 18227200 | tf_op jit(solution)/shard_map/while/body/eval_jaxpr/hqk,khd->qhd/dot_general | solution.py:145
  475.4 12.6 %fusion.73 = bf16[2,64,1024]{2,1,0:T(8,128)(2,1)} fusion(f32[2,64,1024]{2,1,0:T(8,128)} %fusion.22, f32[2,512,1024]{2,1,0:T(8,128)} %fusion.142, bf16[1024,3,2,64]{0,3,2,1:T(8,128)(2,1)} %squeeze.98, f32[2,512,1024]{2,1,0:T(8,128)} %copy-done.30, f32[2,512]{1,0:T(2,128)S(1)} %log_add_fusion, pred[512,1024]{1,0:T(8,128)(4,1)S(1)} %copy-done.21), kind=kOutput, calls=%fused_computation.95 | convolution fusion | flops 146016256 | bytes 18751488 | tf_op jit(solution)/shard_map/while/body/eval_jaxpr/hqk,qhd->khd/dot_general | solution.py:147
  493.6 4.1 pad_maximum_fusion.2
  497.7 6.3 all-to-all-start.5
  506.3 3.8 convolution_convert_fusion
  510.1 4.5 copy.134
  514.6 6.4 reshape.1072
  542.6 4.2 all-to-all-start.6
  546.8 3.9 convolution_convert_fusion.1
  553.6 3.6 fusion.110
  557.1 3.7 fusion.139
  560.9 13.1 %fusion.34 = f32[2,64,1024]{2,1,0:T(8,128)} fusion(f32[2,512,1024]{2,1,0:T(8,128)} %fusion.139, bf16[1024,3,2,64]{0,3,2,1:T(8,128)(2,1)} %copy-done.40, f32[2,512,1024]{2,1,0:T(8,128)} %copy-done.29, f32[2,512]{1,0:T(2,128)S(1)} %log_add_fusion.3, pred[512,1024]{1,0:T(8,128)(4,1)} %get-tuple-element.156), kind=kOutput, calls=%fused_computation.43 | convolution fusion | flops 145754112 | bytes 18489344 | tf_op jit(solution)/shard_map/while/body/eval_jaxpr/hqk,qhd->khd/dot_general | solution.py:147
  574.0 12.8 %fusion.97 = bf16[512,2,64]{0,2,1:T(8,128)(2,1)} fusion(f32[2,512,1024]{2,1,0:T(8,128)} %fusion.139, bf16[1024,3,2,64]{0,3,2,1:T(8,128)(2,1)} %copy-done.40, f32[2,512,1024]{2,1,0:T(8,128)} %copy-done.29, f32[2,512]{1,0:T(2,128)S(1)} %log_add_fusion.3, pred[512,1024]{1,0:T(8,128)(4,1)} %get-tuple-element.156), kind=kOutput, calls=%fused_computation.111 | convolution fusion | flops 145819648 | bytes 18227200 | tf_op jit(solution)/shard_map/while/body/eval_jaxpr/hqk,khd->qhd/dot_general | solution.py:145
  587.0 3.8 fusion.138
  592.8 12.3 %fusion.100 = bf16[512,2,64]{0,2,1:T(8,128)(2,1)} fusion(f32[2,512,1024]{2,1,0:T(8,128)} %fusion.138, bf16[1024,3,2,64]{0,3,2,1:T(8,128)(2,1)} %copy-done.40, f32[2,512,1024]{2,1,0:T(8,128)} %copy-done.27, f32[2,512]{1,0:T(2,128)S(1)} %log_add_fusion.2, pred[512,1024]{1,0:T(8,128)(4,1)S(1)} %copy-done.21), kind=kOutput, calls=%fused_computation.112 | convolution fusion | flops 145819648 | bytes 18227200 | tf_op jit(solution)/shard_map/while/body/eval_jaxpr/hqk,khd->qhd/dot_general | solution.py:145
  605.1 12.0 %fusion.76 = bf16[2,64,1024]{2,1,0:T(8,128)(2,1)S(1)} fusion(f32[2,64,1024]{2,1,0:T(8,128)} %fusion.34, f32[2,512,1024]{2,1,0:T(8,128)} %fusion.138, bf16[1024,3,2,64]{0,3,2,1:T(8,128)(2,1)} %copy-done.40, f32[2,512,1024]{2,1,0:T(8,128)} %copy-done.27, f32[2,512]{1,0:T(2,128)S(1)} %log_add_fusion.2, pred[512,1024]{1,0:T(8,128)(4,1)S(1)} %copy-done.21), kind=kOutput, calls=%fused_computation.96 | convolution fusion | flops 146016256 | bytes 18751488 | tf_op jit(solution)/shard_map/while/body/eval_jaxpr/hqk,qhd->khd/dot_general | solution.py:147
  619.6 3.8 pad_maximum_fusion.3
  623.4 4.6 all-to-all-start.7
  629.3 4.9 copy.133
  634.3 6.5 reshape.1067
  651.8 4.4 reshape.1065
  669.9 23.6 %convert_element_type.303 = bf16[8,4,196928]{2,1,0:T(4,128)(2,1)} reshape(bf16[6301696]{0:T(1024)(128)(2,1)} %constant_dynamic-update-slice_fusion) | data formatting | bytes 25206784 | tf_op jit(solution)/shard_map/convert_element_type | solution.py:341
  693.5 11.5 %copy.135 = bf16[8,4,196928]{2,0,1:T(8,128)(2,1)} copy(bf16[8,4,196928]{2,1,0:T(4,128)(2,1)} %convert_element_type.303) | data formatting | bytes 25206784 | tf_op jit(solution)/shard_map/convert_element_type | solution.py:341
  705.1 98.9 %reduce-scatter.4.cloned.1.call-done = bf16[8,1,196928]{2,0,1:T(8,128)(2,1)} async-done(((bf16[8,4,196928]{2,0,1:T(8,128)(2,1)}), bf16[8,1,196928]{2,0,1:T(8,128)(2,1)}) %reduce-scatter.4.cloned.1.call-update) | async-done | bytes 3150864
  804.0 6.9 copy.136
  815.1 208.4 %all-reduce.10.cloned.1.call-done = f32[8,1,196928]{2,1,0:T(1,128)} async-done(((f32[8,1,196928]{2,1,0:T(1,128)}), f32[8,1,196928]{2,1,0:T(1,128)}) %all-reduce.10.cloned.1.call-update) | async-done | bytes 6301712
  1023.6 3.9 multiply_reduce_fusion.5
  1028.9 6.8 all-reduce.4
  1035.6 19.4 %all-reduce.3 = (f32[]{:T(128)}, f32[2,2,512]{2,1,0:T(2,128)}) all-reduce(f32[]{:T(128)} %get-tuple-element.78, f32[2,2,512]{2,1,0:T(2,128)S(1)} %get-tuple-element.79), channel_id=1, replica_groups=mesh['dp'=8,'sp'=4] {'dp'}, use_global_device_ids=true, to_apply=%region_28.29 | all-reduce | flops 2049 | bytes 16392 | tf_op jit(solution)/shard_map/psum | solution.py:257
  1055.8 9.0 multiply_reduce_fusion.4
  (292 shorter events, 173.9 us)
Async XLA Ops:
  7.2 245.9 %all-reduce.8.cloned.1.call-start = ((), (), s32[]{:S(2)}) async-start(), calls=%async_computation.9 | async-start | bytes 25206784
  256.3 2.5 copy-start.37
  260.8 43.0 %all-to-all-start = ((bf16[1,256,3,4,128]{1,4,2,0,3:T(8,128)(2,1)}), bf16[1,256,3,4,128]{1,4,2,0,3:T(8,128)(2,1)}, u32[]{:S(2)}, u32[]{:S(2)}) async-start(bf16[1,256,3,4,128]{1,4,2,0,3:T(8,128)(2,1)} %pad_maximum_fusion.8), calls=%async_computation | async-start | bytes 1572864 | tf_op jit(solution)/shard_map/all_to_all | solution.py:173
  287.7 18.4 %copy-start.21 = (pred[512,1024]{1,0:T(8,128)(4,1)S(1)}, pred[512,1024]{1,0:T(8,128)(4,1)}, u32[]{:S(2)}) copy-start(pred[512,1024]{1,0:T(8,128)(4,1)} %get-tuple-element.157) | copy-start | bytes 1572868
  289.1 37.0 %copy-start.25 = (bf16[512,512]{1,0:T(8,128)(2,1)}, bf16[512,512]{1,0:T(8,128)(2,1)S(1)}, u32[]{:S(2)}) copy-start(bf16[512,512]{1,0:T(8,128)(2,1)S(1)} %slice.333) | copy-start | bytes 1572868
  306.1 6.1 copy-start.40
  307.2 2.5 copy-start.27
  311.0 2.5 copy-start.29
  313.5 12.7 %copy-start.38 = (bf16[1,256,512]{2,1,0:T(8,128)(2,1)S(1)}, bf16[1,256,512]{2,1,0:T(8,128)(2,1)}, u32[]{:S(2)}) copy-start(bf16[1,256,512]{2,1,0:T(8,128)(2,1)} %param.6) | copy-start | bytes 786436
  317.9 7.8 all-to-all-start.1
  326.1 4.2 copy-start.35
  326.6 3.8 copy-start.17
  329.9 3.1 copy-start.4
  329.9 2.4 copy-start.14
  351.7 2.2 copy-start.41
  353.9 4.5 copy-start.30
  359.8 3.5 copy-start.32
  371.0 18.2 %all-to-all-start.3 = ((bf16[4,2,16384]{2,1,0:T(2,128)(2,1)}), bf16[4,2,16384]{2,1,0:T(2,128)(2,1)}, u32[]{:S(2)}, u32[]{:S(2)}) async-start(bf16[4,2,16384]{2,1,0:T(2,128)(2,1)} %reshape.1086), calls=%async_computation.3 | async-start | bytes 524288 | tf_op jit(solution)/shard_map/all_to_all | solution.py:179
  378.5 14.5 %copy-start.23 = (bf16[512,512]{1,0:T(8,128)(2,1)}, bf16[512,512]{1,0:T(8,128)(2,1)S(1)}, u32[]{:S(2)}) copy-start(bf16[512,512]{1,0:T(8,128)(2,1)S(1)} %slice.359) | copy-start | bytes 1572868
  392.9 4.7 copy-start.15
  392.9 4.7 copy-start.42
  416.4 4.5 copy-start.51
  454.0 3.9 copy-start.31
  454.0 3.9 copy-start.50
  497.7 27.0 %all-to-all-start.5 = ((bf16[1,1024,3,1,128]{4,2,3,0,1:T(4,128)(2,1)}), bf16[1,1024,3,1,128]{4,2,3,0,1:T(4,128)(2,1)}, u32[]{:S(2)}, u32[]{:S(2)}) async-start(bf16[1,1024,3,1,128]{4,2,3,0,1:T(4,128)(2,1)} %pad_maximum_fusion.2), calls=%async_computation.5 | async-start | bytes 2097152 | tf_op jit(solution)/shard_map/all_to_all | solution.py:203
  532.0 2.5 copy-start.18
  534.5 2.3 copy-start.2
  535.4 2.7 copy-start.48
  535.4 2.7 copy-start.49
  538.1 89.9 %copy-start.8 = (f32[1,256,512]{2,1,0:T(8,128)}, f32[1,256,512]{2,1,0:T(8,128)S(1)}, u32[]{:S(2)}) copy-start(f32[1,256,512]{2,1,0:T(8,128)S(1)} %multiply_subtract_fusion) | copy-start | bytes 1572868
  542.6 9.7 all-to-all-start.6
  546.8 3.9 copy-start.45
  587.0 3.8 copy-start.28
  617.1 11.0 %copy-start.36 = (bf16[1,256,4,1,128]{1,4,2,3,0:T(8,128)(2,1)S(1)}, bf16[1,256,4,1,128]{1,4,2,3,0:T(8,128)(2,1)}, u32[]{:S(2)}) copy-start(bf16[1,256,4,1,128]{1,4,2,3,0:T(8,128)(2,1)} %copy-done.35) | copy-start | bytes 786436
  623.4 23.1 %all-to-all-start.7 = ((bf16[1,1024,3,1,128]{4,2,3,0,1:T(4,128)(2,1)}), bf16[1,1024,3,1,128]{4,2,3,0,1:T(4,128)(2,1)}, u32[]{:S(2)}, u32[]{:S(2)}) async-start(bf16[1,1024,3,1,128]{4,2,3,0,1:T(4,128)(2,1)} %pad_maximum_fusion.3), calls=%async_computation.7 | async-start | bytes 2097152 | tf_op jit(solution)/shard_map/all_to_all | solution.py:203
  628.0 176.0 %reduce-scatter.4.cloned.1.call-start = ((), (), s32[]{:S(2)}) async-start(), calls=%async_computation.11 | async-start | bytes 15759360
  634.3 6.6 copy-start.16
  634.3 8.4 copy-start.34
  651.8 9.1 copy-start.7
  656.2 6.4 copy-start.20
  660.9 3.5 copy-start.13
  662.6 3.1 copy-start.43
  662.6 3.9 copy-start.6
  664.4 3.8 copy-start.19
  705.0 318.5 %all-reduce.10.cloned.1.call-start = ((), (), s32[]{:S(2)}) async-start(), calls=%async_computation.10 | async-start | bytes 12607488
  810.9 216.6 %copy-start.1 = (bf16[512,1536]{1,0:T(8,128)(2,1)S(1)}, bf16[512,1536]{1,0:T(8,128)(2,1)}, u32[]{:S(2)}) copy-start(bf16[512,1536]{1,0:T(8,128)(2,1)} %copy-done) | copy-start | bytes 4718596
  810.9 216.6 %copy-start.9 = (f32[1,256,512]{2,1,0:T(8,128)S(1)}, f32[1,256,512]{2,1,0:T(8,128)}, u32[]{:S(2)}) copy-start(f32[1,256,512]{2,1,0:T(8,128)} %copy-done.8) | copy-start | bytes 1572868
  810.9 216.6 %copy-start.11 = (bf16[1,256,3,8,64]{1,4,3,2,0:T(8,128)(2,1)S(1)}, bf16[1,256,3,8,64]{1,4,3,2,0:T(8,128)(2,1)}, u32[]{:S(2)}) copy-start(bf16[1,256,3,8,64]{1,4,3,2,0:T(8,128)(2,1)} %copy-done.10) | copy-start | bytes 2359300
  (14 other events, 19.5 us)
Sparse Core Ops, SparseCore 0:
  20.5 232.5 all-reduce.7
  705.1 98.7 reduce-scatter.3
  811.1 212.4 all-reduce.9
